TPU v7x, 32 devices: a whole 2x2x4 slice. The times are simulated.
32 devices in a mesh: groups: 2 (over x), seq: 16 (over z, y, core).
Axes of the slice: x: 2, y: 2, z: 4, core: 2. Of those that a mesh axis runs over, the one named last changes fastest.
Arguments:
- visual: bfloat16 [32768, 1152], P(('groups', 'seq')), parts along dimension 0, may hold values from -18 to 18
- vis_proj: bfloat16 [1152, 1792], replicated, may hold values from -0.1875 to 0.1875
- kv_proj: bfloat16 [1792, 512], replicated, may hold values from -0.125 to 0.125
- out_proj: bfloat16 [1792, 1792], P(None, 'seq'), may hold values from -0.125 to 0.125
- queries: bfloat16 [256, 1792], P(('groups', 'seq')), parts along dimension 0, may hold values from -350 to 350
- frame_range: int32 [2, 2], P('groups'), parts along dimension 0, may hold values from 0 to 64, as said below
- text_lens: int32 [2], P('groups'), parts along dimension 0, may hold values from 1 to 128, as said below
Outputs:
- attended: bfloat16 [256, 1792], P(('groups', 'seq')), parts along dimension 0
There are 2 independent parts, one for each index of `groups`. A program takes and returns all parts, laid end to end along the dimension named above; an argument that names none is the same for every part. Nothing has to cross between parts.
Inputs may be any that keep to these rules, and one draw needn't show every extreme that they name: frame_range[b, 0] < frame_range[b, 1] for every block b; some block attends all 64 frames. `text_lens`: some block is full.
All inputs are finite; a program needn't handle non-finite values.
Results may differ from a plain program's by a relative error of at most 0.02.
The roundings to bfloat16 on the way count: a program that leaves them out, or rounds other values in their place, can miss the bound.
Values may be sent and summed in bfloat16 or wider, within the bound.
A program may use at most 128 MiB of HBM per device.

v0:
```python
import jax
import jax.numpy as jnp
from jax import lax
from jax.sharding import PartitionSpec as P

HEADS = 14
KV_HEADS = 2
HEAD_DIM = 128
FRAME_TOK = 256
QBLK = 128
NEG = -1e30


def fresh_state(row_count):
    return (
        jnp.zeros((row_count, HEADS * HEAD_DIM), jnp.float32),
        jnp.full((row_count, HEADS), NEG, jnp.float32),
        jnp.zeros((row_count, HEADS), jnp.float32),
    )


def absorb(running, query_rows, key_rows, value_rows, allowed):
    output_sum, maxima, totals = running
    row_count = query_rows.shape[0]
    group_size = HEADS // KV_HEADS
    query_heads = query_rows.reshape(row_count, KV_HEADS, group_size, HEAD_DIM)
    scores = jnp.einsum(
        "tkgd,rkd->tkgr", query_heads, key_rows, preferred_element_type=jnp.float32
    ) * HEAD_DIM ** (-0.5)
    masked = jnp.where(allowed, scores, NEG)
    new_maxima = jnp.maximum(maxima, jnp.max(masked, axis=-1).reshape(row_count, HEADS))
    shaped = new_maxima.reshape(row_count, KV_HEADS, group_size)
    weights = jnp.where(allowed, jnp.exp(scores - shaped[..., None]), 0.0)
    new_totals = jnp.sum(weights, axis=-1).reshape(row_count, HEADS)
    blended = jnp.einsum(
        "tkgr,rkd->tkgd",
        weights.astype(jnp.bfloat16),
        value_rows,
        preferred_element_type=jnp.float32,
    )
    new_sum = blended.reshape(row_count, HEADS, HEAD_DIM)
    return (new_sum.reshape(row_count, HEADS * HEAD_DIM), new_maxima, new_totals)


def visit_keys(running, query_rows, key_rows, value_rows, frame_range, block_id, first_row):
    local_count = key_rows.shape[0]
    bounds = lax.dynamic_index_in_dim(frame_range, block_id, 0, keepdims=False)
    frames = (first_row + jnp.arange(local_count, dtype=jnp.int32)) // FRAME_TOK
    allowed = (frames >= bounds[0]) & (frames < bounds[1])
    result = absorb(running, query_rows, key_rows, value_rows, allowed)
    return result


def body(visual, vis_proj, kv_proj, out_proj, queries, frame_range, text_lens):
    devices = lax.axis_size("seq")
    my_index = lax.axis_index("seq")
    hidden = jax.nn.gelu(
        jnp.dot(visual, vis_proj, preferred_element_type=jnp.float32), approximate=True
    ).astype(jnp.bfloat16)
    key_value = jnp.dot(hidden, kv_proj, preferred_element_type=jnp.float32).astype(jnp.bfloat16)
    kv_width = KV_HEADS * HEAD_DIM
    local_count = visual.shape[0]
    key_rows = key_value[:, :kv_width].reshape(local_count, KV_HEADS, HEAD_DIM)
    value_rows = key_value[:, kv_width:].reshape(local_count, KV_HEADS, HEAD_DIM)
    first_row = my_index * local_count
    own_count = queries.shape[0]

    def visit_local(running, query_rows, block_id):
        return visit_keys(
            running, query_rows, key_rows, value_rows, frame_range, block_id, first_row
        )

    every_query = lax.all_gather(queries, "seq", axis=0, tiled=True)
    block_count = every_query.shape[0] // QBLK
    stacked = every_query.reshape(block_count, QBLK, HEADS * HEAD_DIM)

    def one_block(packed):
        block_rows, block_id = packed
        return visit_local(fresh_state(QBLK), block_rows, block_id)

    sums_all, maxima_all, totals_all = lax.map(
        one_block, (stacked, jnp.arange(block_count, dtype=jnp.int32))
    )
    part_sums, part_maxima, part_totals = (
        lax.all_to_all(
            sums_all.reshape(1, block_count * QBLK, HEADS * HEAD_DIM),
            "seq",
            split_axis=1,
            concat_axis=0,
            tiled=True,
        ),
        lax.all_to_all(
            maxima_all.reshape(1, block_count * QBLK, HEADS),
            "seq",
            split_axis=1,
            concat_axis=0,
            tiled=True,
        ),
        lax.all_to_all(
            totals_all.reshape(1, block_count * QBLK, HEADS),
            "seq",
            split_axis=1,
            concat_axis=0,
            tiled=True,
        ),
    )
    maxima = jnp.max(part_maxima, axis=0)
    scaling = jnp.exp(part_maxima - maxima[None])
    totals = jnp.sum(scaling * part_totals, axis=0)
    weighted = part_sums.reshape(devices, own_count, HEADS, HEAD_DIM) * scaling[..., None]
    output_sum = jnp.sum(weighted, axis=0).reshape(own_count, HEADS * HEAD_DIM)
    normed = output_sum.reshape(own_count, HEADS, HEAD_DIM) / totals[..., None]
    my_block = my_index * own_count // QBLK
    length = lax.dynamic_index_in_dim(text_lens, my_block, 0, keepdims=False)
    positions = my_index * own_count % QBLK + jnp.arange(own_count, dtype=jnp.int32)
    attention = (
        jnp.where((positions < length)[:, None, None], normed, 0.0)
        .reshape(own_count, HEADS * HEAD_DIM)
        .astype(jnp.bfloat16)
    )
    return jnp.dot(
        attention,
        lax.all_gather(out_proj, "seq", axis=1, tiled=True),
        preferred_element_type=jnp.float32,
    ).astype(jnp.bfloat16)


def solution(mesh):
    placed = (
        P(("groups", "seq"), None),
        P(),
        P(),
        P(None, "seq"),
        P(("groups", "seq"), None),
        P("groups", None),
        P("groups"),
    )
    return jax.shard_map(
        body, mesh=mesh, in_specs=placed, out_specs=P(("groups", "seq"), None), check_vma=False
    )
```

profile of v0, /device:TPU:9, one launch (start us, length us, event | category | flops | bytes accessed | tf_op | source)
XLA Modules:
  0.0 117.4 jit_solution(4725177874971610116)
XLA Ops:
  6.5 0.0 copy-start
  6.5 0.0 all-gather.2.cloned.1.call-start
  6.5 0.7 all-gather.2.cloned.1.call-update
  7.3 22.1 %all_gather.6 = bf16[128,1792]{1,0:T(8,128)(2,1)S(1)} all-gather(bf16[8,1792]{1,0:T(8,128)(2,1)} %param.11), channel_id=1, replica_groups=mesh['groups'=2,'seq'=16] {'seq'}, dimensions={0}, use_global_device_ids=true | all-gather | bytes 487424 | tf_op jit(solution)/shard_map/all_gather | solution.py:73
  29.4 0.3 copy.16
  29.7 1.3 %fusion.39 = (s32[1,1]{1,0:T(1,128)}, s32[1,1]{1,0:T(1,128)}) fusion(s32[1,2]{1,0:T(1,128)} %param.12), kind=kLoop, calls=%fused_computation.51 | loop fusion | bytes 16 | tf_op jit(solution)/shard_map/while/body/eval_jaxpr/slice | solution.py:49
  31.0 1.2 %compare_and_fusion = pred[1024]{0:T(1024)(128)(4,1)S(1)} fusion(s32[]{:T(128)} %bitcast.5, s32[]{:T(128)} %bitcast.4, s32[]{:T(128)S(6)} %mul.69), kind=kLoop, calls=%fused_computation.41 | loop fusion | flops 19456 | bytes 1036 | tf_op jit(solution)/shard_map/while/body/eval_jaxpr/and | solution.py:49
  32.2 0.0 copy-done
  32.2 11.2 %fusion.18 = bf16[1024,512]{0,1:T(8,128)(2,1)} fusion(bf16[1792,512]{1,0:T(8,128)(2,1)} %param.9, bf16[1024,1152]{1,0:T(8,128)(2,1)S(1)} %copy-done, bf16[1152,1792]{1,0:T(8,128)(2,1)} %param.8), kind=kOutput, calls=%fused_computation.20 | convolution fusion | flops 6123945984 | bytes 9371648 | tf_op jit(solution)/shard_map/dot_general | solution.py:60
  43.4 2.1 %fusion.38 = (bf16[1024,256]{0,1:T(8,128)(2,1)S(1)}, bf16[1024,256]{0,1:T(8,128)(2,1)}) fusion(bf16[1024,512]{0,1:T(8,128)(2,1)} %fusion.18), kind=kLoop, calls=%fused_computation.50 | loop fusion | bytes 2097152 | tf_op jit(solution)/shard_map/slice | solution.py:63
  45.5 1.6 %fusion.8 = (f32[128,2,7]{0,2,1:T(8,128)S(1)}, f32[2,1024,128,7]{2,1,3,0:T(8,128)S(1)}) fusion(pred[1024]{0:T(1024)(128)(4,1)S(1)} %compare_and_fusion, bf16[1024,2,128,1]{0,2,3,1:T(8,128)(2,1)S(1)} %bitcast.58, bf16[128,2,7,128]{0,3,2,1:T(8,128)(2,1)S(1)} %bitcast.59), kind=kOutput, calls=%fused_computation.11 | convolution fusion | flops 475265280 | bytes 8331264 | tf_op jit(solution)/shard_map/while/body/eval_jaxpr/tkgd,rkd->tkgr/dot_general | solution.py:27
  47.1 0.0 copy-start.1
  47.1 2.9 %copy-done.1 = f32[2,1024,128,7]{2,1,3,0:T(8,128)} copy-done((f32[2,1024,128,7]{2,1,3,0:T(8,128)}, f32[2,1024,128,7]{2,1,3,0:T(8,128)S(1)}, u32[]{:S(2)}) %copy-start.1) | copy-done | bytes 7340056
  50.1 2.0 %fusion.11 = f32[128,2,7]{0,2,1:T(8,128)S(1)} fusion(f32[2,1024,128,7]{2,1,3,0:T(8,128)S(1)} %get-tuple-element.38, f32[128,2,7]{0,2,1:T(8,128)S(1)} %broadcast_maximum_fusion, pred[1024]{0:T(1024)(128)(4,1)S(1)} %compare_and_fusion), kind=kLoop, calls=%fused_computation.14 | loop fusion | flops 7338240 | bytes 7355392 | tf_op jit(solution)/shard_map/while/body/eval_jaxpr/reduce_sum | solution.py:34
  52.0 0.7 copy.24
  52.8 6.3 %all-to-all-start.2 = ((f32[1,128,14]{2,0,1:T(1,128)}), f32[1,128,14]{2,0,1:T(1,128)S(1)}, u32[]{:S(2)}, u32[]{:S(2)}) async-start(f32[1,128,14]{2,0,1:T(1,128)} %copy.24), calls=%async_computation.2 | async-start | bytes 131072 | tf_op jit(solution)/shard_map/all_to_all | solution.py:99
  59.1 0.7 copy.21
  59.8 4.5 %all-to-all-done.2 = f32[1,128,14]{2,0,1:T(1,128)S(1)} async-done(((f32[1,128,14]{2,0,1:T(1,128)}), f32[1,128,14]{2,0,1:T(1,128)S(1)}, u32[]{:S(2)}, u32[]{:S(2)}) %all-to-all-start.2) | async-done | bytes 7200 | tf_op jit(solution)/shard_map/all_to_all | solution.py:99
  64.3 5.4 %all-to-all-start.1 = ((f32[1,128,14]{2,0,1:T(1,128)}), f32[1,128,14]{2,0,1:T(1,128)S(1)}, u32[]{:S(2)}, u32[]{:S(2)}) async-start(f32[1,128,14]{2,0,1:T(1,128)} %copy.21), calls=%async_computation.1 | async-start | bytes 131072 | tf_op jit(solution)/shard_map/all_to_all | solution.py:92
  69.7 4.8 %fusion.13 = f32[2,128,128,7]{2,1,3,0:T(8,128)S(1)} fusion(bf16[1024,2,128,1]{0,2,3,1:T(8,128)(2,1)} %bitcast.63, f32[2,1024,128,7]{2,1,3,0:T(8,128)} %copy-done.1, f32[128,2,7]{0,2,1:T(8,128)S(1)} %broadcast_maximum_fusion, pred[1024]{0:T(1024)(128)(4,1)S(1)} %compare_and_fusion), kind=kOutput, calls=%fused_computation.16 | convolution fusion | flops 477102080 | bytes 8790016 | tf_op jit(solution)/shard_map/while/body/eval_jaxpr/tkgr,rkd->tkgd/dot_general | solution.py:35
  74.5 2.1 %copy.20 = f32[1,128,1792]{2,0,1:T(1,128)} copy(f32[1,128,1792]{1,2,0:T(8,128)S(1)} %bitcast.60) | data formatting | bytes 1835008 | tf_op jit(solution)/shard_map/while/body/jit(dynamic_update_index_in_dim)/broadcast_in_dim | solution.py:81
  76.6 0.0 all-to-all-done.1
  76.6 6.2 %all-to-all-start = ((f32[1,128,1792]{2,0,1:T(1,128)}), f32[1,128,1792]{2,0,1:T(1,128)S(1)}, u32[]{:S(2)}, u32[]{:S(2)}) async-start(f32[1,128,1792]{2,0,1:T(1,128)} %copy.20), calls=%async_computation | async-start | bytes 1835008 | tf_op jit(solution)/shard_map/all_to_all | solution.py:85
  83.4 0.2 copy.33
  83.6 0.8 copy.32
  84.5 0.1 copy.35
  84.6 0.9 multiply_reduce_fusion
  85.6 19.4 %all-to-all-done = f32[1,128,1792]{2,0,1:T(1,128)S(1)} async-done(((f32[1,128,1792]{2,0,1:T(1,128)}), f32[1,128,1792]{2,0,1:T(1,128)S(1)}, u32[]{:S(2)}, u32[]{:S(2)}) %all-to-all-start) | async-done | bytes 917536 | tf_op jit(solution)/shard_map/all_to_all | solution.py:85
  105.0 0.3 fusion.21
  105.3 0.0 all-gather.2.cloned.1.call-done
  105.3 5.2 %convolution_convert_fusion = bf16[8,1792]{1,0:T(8,128)(2,1)} fusion(bf16[1792,1792]{0,1:T(8,128)(2,1)} %all-gather.2.cloned.1.call-done, f32[8,1792]{1,0:T(8,128)S(1)} %fusion.21, f32[8,14]{0,1:T(8,128)S(1)} %get-tuple-element.21, pred[8]{0:T(512)(128)(4,1)S(1)} %add_compare_fusion), kind=kOutput, calls=%fused_computation.19 | convolution fusion | flops 51437568 | bytes 6509000 | tf_op jit(solution)/shard_map/dot_general | solution.py:121
  (6 shorter events, 0.1 us)
Async XLA Ops:
  6.5 25.7 %copy-start = (bf16[1024,1152]{1,0:T(8,128)(2,1)S(1)}, bf16[1024,1152]{1,0:T(8,128)(2,1)}, u32[]{:S(2)}) copy-start(bf16[1024,1152]{1,0:T(8,128)(2,1)} %param.7) | copy-start | bytes 7077892
  6.5 98.8 %all-gather.2.cloned.1.call-start = ((), (), s32[]{:S(2)}) async-start(), calls=%async_computation.3 | async-start | bytes 6823936 | tf_op jit(solution)/shard_map/all_gather | solution.py:123
  47.1 3.0 %copy-start.1 = (f32[2,1024,128,7]{2,1,3,0:T(8,128)}, f32[2,1024,128,7]{2,1,3,0:T(8,128)S(1)}, u32[]{:S(2)}) copy-start(f32[2,1024,128,7]{2,1,3,0:T(8,128)S(1)} %get-tuple-element.38) | copy-start | bytes 22020100
  52.8 11.5 %all-to-all-start.2 = ((f32[1,128,14]{2,0,1:T(1,128)}), f32[1,128,14]{2,0,1:T(1,128)S(1)}, u32[]{:S(2)}, u32[]{:S(2)}) async-start(f32[1,128,14]{2,0,1:T(1,128)} %copy.24), calls=%async_computation.2 | async-start | bytes 131072 | tf_op jit(solution)/shard_map/all_to_all | solution.py:99
  64.3 12.3 %all-to-all-start.1 = ((f32[1,128,14]{2,0,1:T(1,128)}), f32[1,128,14]{2,0,1:T(1,128)S(1)}, u32[]{:S(2)}, u32[]{:S(2)}) async-start(f32[1,128,14]{2,0,1:T(1,128)} %copy.21), calls=%async_computation.1 | async-start | bytes 131072 | tf_op jit(solution)/shard_map/all_to_all | solution.py:92
  76.6 28.4 %all-to-all-start = ((f32[1,128,1792]{2,0,1:T(1,128)}), f32[1,128,1792]{2,0,1:T(1,128)S(1)}, u32[]{:S(2)}, u32[]{:S(2)}) async-start(f32[1,128,1792]{2,0,1:T(1,128)} %copy.20), calls=%async_computation | async-start | bytes 1835008 | tf_op jit(solution)/shard_map/all_to_all | solution.py:85
Sparse Core Ops, SparseCore 0:
  9.6 64.7 all-gather.1
where the time goes:
time: 118 us; the launch traced here: 117 us
  waiting for transfers between devices  24.6 us (21%)
  matrix products  22.8 us (19%)
  blocking collectives  22.1 us (19%)
  starting transfers between devices  17.9 us (15%)
  between operations  14.1 us (12%)
  local copies, waits for them, and re-layouts  11.3 us (10%)
  other arithmetic  4.46 us (4%)
    all_gather x1, blocking collectives, body(): every_query = lax.all_gather(queries, 'seq', axis=0, tiled=True)  22.1 us
    all_to_all x1, waiting for transfers between devices, body(): lax.all_to_all(sums_all.reshape(1, block_count * QBLK, HEADS * HEAD_DIM),...  19.4 us
    dot_general x1, matrix products, body(): jnp.dot(hidden, kv_proj, preferred_element_type=jnp.float32)  11.2 us
    all_to_all x1, starting transfers between devices, body(): lax.all_to_all(totals_all.reshape(1, block_count * QBLK, HEADS), 'seq', s...  6.29 us
    all_to_all x1, starting transfers between devices, body(): lax.all_to_all(sums_all.reshape(1, block_count * QBLK, HEADS * HEAD_DIM),...  6.16 us
    all_to_all x1, starting transfers between devices, body(): lax.all_to_all(maxima_all.reshape(1, block_count * QBLK, HEADS), 'seq', s...  5.45 us
    dot_general x1, matrix products, body(): jnp.dot(attention, lax.all_gather(out_proj, 'seq', axis=1, tiled=True), p...  5.24 us
    dot_general x1, matrix products, absorb(): jnp.einsum('tkgr,rkd->tkgd', weights.astype(jnp.bfloat16), value_rows, pr...  4.78 us
  transfers between devices with their start and end apart: 4, of which 2 were waited for; matrix products, arithmetic and copies ran while one was open for 26% of the time, Pallas kernels for 0%

commit v1 on v0

--- a/solution.py
+++ b/solution.py
@@ -96,12 +96,20 @@
             concat_axis=0,
             tiled=True,
         ),
-        lax.all_to_all(
-            totals_all.reshape(1, block_count * QBLK, HEADS),
-            "seq",
-            split_axis=1,
-            concat_axis=0,
-            tiled=True,
+        jnp.concatenate(
+            lax.all_to_all(
+                jnp.stack(
+                    jnp.split(
+                        totals_all.reshape(1, block_count * QBLK, HEADS),
+                        lax.axis_size("seq"),
+                        axis=1,
+                    )
+                ),
+                "seq",
+                0,
+                0,
+            ),
+            axis=0,
         ),
     )
     maxima = jnp.max(part_maxima, axis=0)

time: 118 us -> 128 us (1.085)
  local copies, waits for them, and re-layouts: 11.3 us -> 21.4 us
    unnamed x5 -> x20, local copies, waits for them, and re-layouts: 3.04 us -> 11.9 us
    split x0 -> x17, local copies, waits for them, and re-layouts: none -> 1.35 us  [body(): jnp.split(totals_all.reshape(1, block_count * QBLK, HEADS), lax.axis_size...]
    broadcast_in_dim x3 -> x2, local copies, waits for them, and re-layouts: 2.83 us -> 2.09 us  [body(): lax.map(one_block, (stacked, jnp.arange(block_count, dtype=jnp.int32)))]
  transfers between devices with their start and end apart: 4 -> 4, of which waited for: 2 -> 2; matrix products, arithmetic and copies ran while one was open for 26% -> 32% of each run, Pallas kernels for 0% -> 0%
where the time goes in v1:
time: 128 us; the launch traced here: 127 us
  waiting for transfers between devices  24.5 us (19%)
  matrix products  22.7 us (18%)
  blocking collectives  22.1 us (17%)
  local copies, waits for them, and re-layouts  21.4 us (17%)
  starting transfers between devices  17.6 us (14%)
  between operations  14.2 us (11%)
  other arithmetic  4.54 us (4%)
    all_gather x1, blocking collectives, body(): every_query = lax.all_gather(queries, 'seq', axis=0, tiled=True)  22.1 us
    all_to_all x1, waiting for transfers between devices, body(): lax.all_to_all(sums_all.reshape(1, block_count * QBLK, HEADS * HEAD_DIM),...  19.4 us
    unnamed x20, local copies, waits for them, and re-layouts  11.9 us
    dot_general x1, matrix products, body(): jnp.dot(hidden, kv_proj, preferred_element_type=jnp.float32)  11.2 us
    all_to_all x1, starting transfers between devices, body(): lax.all_to_all(jnp.stack(jnp.split(totals_all.reshape(1, block_count * QB...  6.3 us
    all_to_all x1, starting transfers between devices, body(): lax.all_to_all(sums_all.reshape(1, block_count * QBLK, HEADS * HEAD_DIM),...  6.08 us
    dot_general x1, matrix products, body(): jnp.dot(attention, lax.all_gather(out_proj, 'seq', axis=1, tiled=True), p...  5.24 us
    all_to_all x1, starting transfers between devices, body(): lax.all_to_all(maxima_all.reshape(1, block_count * QBLK, HEADS), 'seq', s...  5.23 us
  transfers between devices with their start and end apart: 4, of which 2 were waited for; matrix products, arithmetic and copies ran while one was open for 32% of the time, Pallas kernels for 0%

profile of v1, /device:TPU:9, one launch (start us, length us, event | category | flops | bytes accessed | tf_op | source)
XLA Modules:
  0.0 127.1 jit_solution(8368570343287911323)
XLA Ops:
  6.5 0.7 all-gather.2.cloned.1.call-update
  7.3 22.1 %all_gather.6 = bf16[128,1792]{1,0:T(8,128)(2,1)S(1)} all-gather(bf16[8,1792]{1,0:T(8,128)(2,1)} %param.11), channel_id=1, replica_groups=mesh['groups'=2,'seq'=16] {'seq'}, dimensions={0}, use_global_device_ids=true | all-gather | bytes 487424 | tf_op jit(solution)/shard_map/all_gather | solution.py:73
  29.4 0.3 copy.73
  29.7 1.3 %fusion.41 = (s32[1,1]{1,0:T(1,128)}, s32[1,1]{1,0:T(1,128)}) fusion(s32[1,2]{1,0:T(1,128)} %param.12), kind=kLoop, calls=%fused_computation.69 | loop fusion | bytes 16 | tf_op jit(solution)/shard_map/while/body/eval_jaxpr/slice | solution.py:49
  31.0 1.3 %compare_and_fusion = pred[1024]{0:T(1024)(128)(4,1)S(1)} fusion(s32[]{:T(128)} %bitcast.5, s32[]{:T(128)} %bitcast.4, s32[]{:T(128)S(6)} %mul.66), kind=kLoop, calls=%fused_computation.58 | loop fusion | flops 19456 | bytes 1036 | tf_op jit(solution)/shard_map/while/body/eval_jaxpr/and | solution.py:49
  32.3 11.2 %fusion.18 = bf16[1024,512]{0,1:T(8,128)(2,1)} fusion(bf16[1792,512]{1,0:T(8,128)(2,1)} %param.9, bf16[1024,1152]{1,0:T(8,128)(2,1)S(1)} %copy-done, bf16[1152,1792]{1,0:T(8,128)(2,1)} %param.8), kind=kOutput, calls=%fused_computation.20 | convolution fusion | flops 6123945984 | bytes 9371648 | tf_op jit(solution)/shard_map/dot_general | solution.py:60
  43.5 2.1 %fusion.39 = (bf16[1024,256]{0,1:T(8,128)(2,1)S(1)}, bf16[1024,256]{0,1:T(8,128)(2,1)}) fusion(bf16[1024,512]{0,1:T(8,128)(2,1)} %fusion.18), kind=kLoop, calls=%fused_computation.67 | loop fusion | bytes 2097152 | tf_op jit(solution)/shard_map/slice | solution.py:63
  45.6 1.6 %fusion.8 = (f32[128,2,7]{0,2,1:T(8,128)S(1)}, f32[2,1024,128,7]{2,1,3,0:T(8,128)S(1)}) fusion(pred[1024]{0:T(1024)(128)(4,1)S(1)} %compare_and_fusion, bf16[1024,2,128,1]{0,2,3,1:T(8,128)(2,1)S(1)} %bitcast.93, bf16[128,2,7,128]{0,3,2,1:T(8,128)(2,1)S(1)} %bitcast.94), kind=kOutput, calls=%fused_computation.11 | convolution fusion | flops 475265280 | bytes 8331264 | tf_op jit(solution)/shard_map/while/body/eval_jaxpr/tkgd,rkd->tkgr/dot_general | solution.py:27
  47.2 2.9 %copy-done.1 = f32[2,1024,128,7]{2,1,3,0:T(8,128)} copy-done((f32[2,1024,128,7]{2,1,3,0:T(8,128)}, f32[2,1024,128,7]{2,1,3,0:T(8,128)S(1)}, u32[]{:S(2)}) %copy-start.1) | copy-done | bytes 7340056
  50.1 2.0 %fusion.11 = f32[128,2,7]{0,2,1:T(8,128)S(1)} fusion(f32[2,1024,128,7]{2,1,3,0:T(8,128)S(1)} %get-tuple-element.55, f32[128,2,7]{0,2,1:T(8,128)S(1)} %broadcast_maximum_fusion, pred[1024]{0:T(1024)(128)(4,1)S(1)} %compare_and_fusion), kind=kLoop, calls=%fused_computation.14 | loop fusion | flops 7338240 | bytes 7355392 | tf_op jit(solution)/shard_map/while/body/eval_jaxpr/reduce_sum | solution.py:34
  52.1 0.1 fusion.40
  52.2 0.1 copy.81
  52.3 0.1 copy.82
  52.4 0.1 copy.83
  52.5 0.1 copy.84
  52.6 0.1 copy.85
  52.6 0.1 copy.86
  53.3 0.1 copy.95
  53.5 0.6 constant_dynamic-update-slice_fusion.15
  54.1 0.6 constant_dynamic-update-slice_fusion.14
  54.7 0.6 constant_dynamic-update-slice_fusion.13
  55.3 0.6 constant_dynamic-update-slice_fusion.12
  55.9 0.6 constant_dynamic-update-slice_fusion.11
  56.5 0.6 constant_dynamic-update-slice_fusion.10
  57.1 0.6 constant_dynamic-update-slice_fusion.9
  57.7 0.6 constant_dynamic-update-slice_fusion.8
  58.2 0.6 constant_dynamic-update-slice_fusion.7
  58.8 0.6 constant_dynamic-update-slice_fusion.6
  59.4 0.6 constant_dynamic-update-slice_fusion.5
  60.0 0.6 constant_dynamic-update-slice_fusion.4
  60.6 0.6 constant_dynamic-update-slice_fusion.3
  61.2 0.6 constant_dynamic-update-slice_fusion.2
  61.8 0.6 constant_dynamic-update-slice_fusion.1
  62.4 0.6 constant_dynamic-update-slice_fusion
  63.0 6.3 %all-to-all-start.2 = ((f32[16,1,8,14]{3,2,1,0:T(8,128)}), f32[16,1,8,14]{3,2,1,0:T(8,128)S(1)}, u32[]{:S(2)}, u32[]{:S(2)}) async-start(f32[16,1,8,14]{3,2,1,0:T(8,128)} %constant_dynamic-update-slice_fusion), calls=%async_computation.2 | async-start | bytes 131072 | tf_op jit(solution)/shard_map/all_to_all | solution.py:100
  69.3 0.7 copy.78
  70.0 4.4 %all-to-all-done.2 = f32[16,1,8,14]{3,2,1,0:T(8,128)S(1)} async-done(((f32[16,1,8,14]{3,2,1,0:T(8,128)}), f32[16,1,8,14]{3,2,1,0:T(8,128)S(1)}, u32[]{:S(2)}, u32[]{:S(2)}) %all-to-all-start.2) | async-done | bytes 7200 | tf_op jit(solution)/shard_map/all_to_all | solution.py:100
  74.4 5.2 %all-to-all-start.1 = ((f32[1,128,14]{2,0,1:T(1,128)}), f32[1,128,14]{2,0,1:T(1,128)S(1)}, u32[]{:S(2)}, u32[]{:S(2)}) async-start(f32[1,128,14]{2,0,1:T(1,128)} %copy.78), calls=%async_computation.1 | async-start | bytes 131072 | tf_op jit(solution)/shard_map/all_to_all | solution.py:92
  79.6 4.7 %fusion.13 = f32[2,128,128,7]{2,1,3,0:T(8,128)S(1)} fusion(bf16[1024,2,128,1]{0,2,3,1:T(8,128)(2,1)} %bitcast.98, f32[2,1024,128,7]{2,1,3,0:T(8,128)} %copy-done.1, f32[128,2,7]{0,2,1:T(8,128)S(1)} %broadcast_maximum_fusion, pred[1024]{0:T(1024)(128)(4,1)S(1)} %compare_and_fusion), kind=kOutput, calls=%fused_computation.16 | convolution fusion | flops 477102080 | bytes 8790016 | tf_op jit(solution)/shard_map/while/body/eval_jaxpr/tkgr,rkd->tkgd/dot_general | solution.py:35
  84.3 2.1 %copy.77 = f32[1,128,1792]{2,0,1:T(1,128)} copy(f32[1,128,1792]{1,2,0:T(8,128)S(1)} %bitcast.95) | data formatting | bytes 1835008 | tf_op jit(solution)/shard_map/while/body/jit(dynamic_update_index_in_dim)/broadcast_in_dim | solution.py:81
  86.4 6.1 %all-to-all-start = ((f32[1,128,1792]{2,0,1:T(1,128)}), f32[1,128,1792]{2,0,1:T(1,128)S(1)}, u32[]{:S(2)}, u32[]{:S(2)}) async-start(f32[1,128,1792]{2,0,1:T(1,128)} %copy.77), calls=%async_computation | async-start | bytes 1835008 | tf_op jit(solution)/shard_map/all_to_all | solution.py:85
  93.1 0.2 copy.104
  93.3 0.1 copy.106
  93.4 0.8 copy.97
  94.3 0.9 fusion.22
  95.2 19.4 %all-to-all-done = f32[1,128,1792]{2,0,1:T(1,128)S(1)} async-done(((f32[1,128,1792]{2,0,1:T(1,128)}), f32[1,128,1792]{2,0,1:T(1,128)S(1)}, u32[]{:S(2)}, u32[]{:S(2)}) %all-to-all-start) | async-done | bytes 917536 | tf_op jit(solution)/shard_map/all_to_all | solution.py:85
  114.7 0.3 fusion.21
  115.0 5.2 %convolution_convert_fusion = bf16[8,1792]{1,0:T(8,128)(2,1)} fusion(bf16[1792,1792]{0,1:T(8,128)(2,1)} %all-gather.2.cloned.1.call-done, f32[8,1792]{1,0:T(8,128)S(1)} %fusion.21, f32[8,14]{0,1:T(8,128)S(1)} %get-tuple-element.21, pred[8]{0:T(512)(128)(4,1)S(1)} %add_compare_fusion), kind=kOutput, calls=%fused_computation.19 | convolution fusion | flops 51437568 | bytes 6509000 | tf_op jit(solution)/shard_map/dot_general | solution.py:129
  (21 shorter events, 0.8 us)
Async XLA Ops:
  6.5 25.8 %copy-start = (bf16[1024,1152]{1,0:T(8,128)(2,1)S(1)}, bf16[1024,1152]{1,0:T(8,128)(2,1)}, u32[]{:S(2)}) copy-start(bf16[1024,1152]{1,0:T(8,128)(2,1)} %param.7) | copy-start | bytes 7077892
  6.5 108.4 %all-gather.2.cloned.1.call-start = ((), (), s32[]{:S(2)}) async-start(), calls=%async_computation.3 | async-start | bytes 6823936 | tf_op jit(solution)/shard_map/all_gather | solution.py:131
  47.2 3.0 %copy-start.1 = (f32[2,1024,128,7]{2,1,3,0:T(8,128)}, f32[2,1024,128,7]{2,1,3,0:T(8,128)S(1)}, u32[]{:S(2)}) copy-start(f32[2,1024,128,7]{2,1,3,0:T(8,128)S(1)} %get-tuple-element.55) | copy-start | bytes 22020100
  63.0 11.4 %all-to-all-start.2 = ((f32[16,1,8,14]{3,2,1,0:T(8,128)}), f32[16,1,8,14]{3,2,1,0:T(8,128)S(1)}, u32[]{:S(2)}, u32[]{:S(2)}) async-start(f32[16,1,8,14]{3,2,1,0:T(8,128)} %constant_dynamic-update-slice_fusion), calls=%async_computation.2 | async-start | bytes 131072 | tf_op jit(solution)/shard_map/all_to_all | solution.py:100
  74.4 12.0 %all-to-all-start.1 = ((f32[1,128,14]{2,0,1:T(1,128)}), f32[1,128,14]{2,0,1:T(1,128)S(1)}, u32[]{:S(2)}, u32[]{:S(2)}) async-start(f32[1,128,14]{2,0,1:T(1,128)} %copy.78), calls=%async_computation.1 | async-start | bytes 131072 | tf_op jit(solution)/shard_map/all_to_all | solution.py:92
  86.4 28.3 %all-to-all-start = ((f32[1,128,1792]{2,0,1:T(1,128)}), f32[1,128,1792]{2,0,1:T(1,128)S(1)}, u32[]{:S(2)}, u32[]{:S(2)}) async-start(f32[1,128,1792]{2,0,1:T(1,128)} %copy.77), calls=%async_computation | async-start | bytes 1835008 | tf_op jit(solution)/shard_map/all_to_all | solution.py:85
Sparse Core Ops, SparseCore 0:
  9.6 64.7 all-gather.1
